TPU v7x, 32 devices: a whole 2x2x4 slice. The times are simulated.
32 devices in a mesh: row: 8 (over z, x), col: 4 (over y, core).
Axes of the slice: x: 2, y: 2, z: 4, core: 2. Of those that a mesh axis runs over, the one named last changes fastest.
Arguments:
- homolog_matrix: bfloat16 [64, 320, 64], P('row', 'col'), may hold values from -6 to 6
- contact_matrix: bfloat16 [320, 320, 128], P('row', 'col'), may hold values from -24 to 24
- genuine_homolog_total: int32 [1], replicated, may hold values from 1 to 64
- genuine_chain_length: int32 [1], replicated, may hold values from 160 to 320
- tensor_product_matrices: bfloat16 [1, 64, 64], replicated, may hold values from -0.75 to 0.75
- tensor_product_final: bfloat16 [1, 1024, 128], replicated, may hold values from -0.75 to 0.75
- mixing_value_gate_matrix: bfloat16 [1, 64, 512], replicated, may hold values from -0.75 to 0.75
- mixing_logit_matrix: bfloat16 [1, 128, 8], replicated
- mixing_final_matrix: bfloat16 [1, 256, 64], replicated, may hold values from -1.5 to 1.5
- feedforward_gate_expand: bfloat16 [1, 128, 1024], replicated, may hold values from -0.5 to 0.5
- feedforward_shrink_matrix: bfloat16 [1, 512, 128], replicated, may hold values from -0.25 to 0.25
Outputs:
- msa_out: bfloat16 [64, 320, 64], P('row', 'col')
- pair_out: bfloat16 [320, 320, 128], P('row', 'col')
Inputs may be any that keep to these rules, and one draw needn't show every extreme that they name: Sequences from genuine_homolog_total on are padding. Residues from genuine_chain_length on are padding.
All inputs are finite; a program needn't handle non-finite values.
Results may differ from a plain program's by a relative error of at most 0.0065.
The roundings to bfloat16 on the way count: a program that leaves them out, or rounds other values in their place, can miss the bound.
Values may be sent and summed in bfloat16 or wider, within the bound.
A program may use at most 64 MiB of HBM per device.

v0:
```python
import jax
import jax.numpy as jnp
from jax import lax
from jax.sharding import PartitionSpec as P

EPSILON = 1e-05
MASKED = -1000000000.0


def broadcast(value, axis, source):
    kept = jnp.where(lax.axis_index(axis) == source, value, 0).astype(value.dtype)
    return lax.psum(kept, axis)


def standardize_features(field):
    field = field.astype(jnp.float32)
    center = field - jnp.mean(field, axis=-1, keepdims=True)
    spread = jnp.mean(center * center, axis=-1, keepdims=True)
    return center * lax.rsqrt(spread + EPSILON)


def local(
    homolog_matrix,
    contact_matrix,
    genuine_homolog_total,
    genuine_chain_length,
    tensor_product_matrices,
    tensor_product_final,
    mixing_value_gate_matrix,
    mixing_logit_matrix,
    mixing_final_matrix,
    feedforward_gate_expand,
    feedforward_shrink_matrix,
):
    homolog_rows_local, chain_positions_local, homolog_rows_full = homolog_matrix.shape
    rows_dev = contact_matrix.shape[0]
    pair_width = contact_matrix.shape[2]
    outer_width = tensor_product_matrices.shape[2] // 2
    head_count = mixing_logit_matrix.shape[2]
    hidden_width = mixing_final_matrix.shape[1]
    head_width = hidden_width // head_count
    trans_width = feedforward_shrink_matrix.shape[1]
    row_blocks = rows_dev // 8
    row_index = lax.axis_index("row")
    col_index = lax.axis_index("col")
    ratio = lax.axis_size("row") // lax.axis_size("col")
    total_seqs = homolog_rows_local * lax.axis_size("row")
    seq_ids = row_index * homolog_rows_local + jnp.arange(homolog_rows_local, dtype=jnp.int32)
    res_ids = col_index * chain_positions_local + jnp.arange(chain_positions_local, dtype=jnp.int32)
    pair_ids = row_index * rows_dev + jnp.arange(rows_dev, dtype=jnp.int32)
    seq_float = (seq_ids < genuine_homolog_total[0]).astype(jnp.float32)
    res_valid = res_ids < genuine_chain_length[0]
    res_float = res_valid.astype(jnp.float32)
    row_float = (pair_ids < genuine_chain_length[0]).astype(jnp.float32)
    divisor = jnp.maximum(
        genuine_homolog_total[0].astype(jnp.float32) * row_float[:, None] * res_float[None, :], 1.0
    )
    starts = jnp.arange(row_blocks, dtype=jnp.int32) * 8
    standardized_source = standardize_features(homolog_matrix).astype(jnp.bfloat16)
    reshaped_tensor = standardized_source.reshape(
        homolog_rows_local * chain_positions_local, homolog_rows_full
    )
    projected = jnp.dot(
        reshaped_tensor, tensor_product_matrices[0], preferred_element_type=jnp.float32
    ).reshape(homolog_rows_local, chain_positions_local, 2 * outer_width)
    projected = (projected * (seq_float[:, None, None] * res_float[None, :, None])).astype(
        jnp.bfloat16
    )
    packed = projected.reshape(homolog_rows_local, chain_positions_local * 2 * outer_width)
    columns = lax.all_gather(packed, "row", axis=0, tiled=True).reshape(
        total_seqs, chain_positions_local, 2 * outer_width
    )
    left_all = columns[:, :, :outer_width].reshape(total_seqs, chain_positions_local * outer_width)
    right = columns[:, :, outer_width:].reshape(total_seqs, chain_positions_local * outer_width)
    left_cols = broadcast(left_all, "col", row_index // ratio).reshape(
        total_seqs, chain_positions_local, outer_width
    )
    left = lax.dynamic_slice_in_dim(left_cols, row_index % ratio * rows_dev, rows_dev, 1)
    outer_weight = tensor_product_final[0]

    def outer_rows(inputs):
        start, pair_rows = inputs
        rows = lax.dynamic_slice_in_dim(left, start, 8, 1).reshape(total_seqs, 8 * outer_width)
        product = lax.dot_general(
            rows, right, (((0,), (0,)), ((), ())), preferred_element_type=jnp.float32
        )
        product = product.reshape(8, outer_width, chain_positions_local, outer_width).transpose(
            0, 2, 1, 3
        )
        product = product.reshape(8, chain_positions_local, outer_width * outer_width)
        scale = lax.dynamic_slice_in_dim(divisor, start, 8, 0)
        outer = (product / scale[:, :, None]).astype(jnp.bfloat16)
        update = jnp.dot(
            outer.reshape(8 * chain_positions_local, outer_width * outer_width),
            outer_weight,
            preferred_element_type=jnp.float32,
        )
        return (
            pair_rows.astype(jnp.float32) + update.reshape(8, chain_positions_local, pair_width)
        ).astype(jnp.bfloat16)

    contact_matrix = lax.map(
        outer_rows,
        (starts, contact_matrix.reshape(row_blocks, 8, chain_positions_local, pair_width)),
    ).reshape(rows_dev, chain_positions_local, pair_width)
    bias_weight = mixing_logit_matrix[0]

    def norm_rows(pair_rows):
        normed_rows = standardize_features(pair_rows).astype(jnp.bfloat16)
        logit_rows = jnp.dot(
            normed_rows.reshape(8 * chain_positions_local, pair_width),
            bias_weight,
            preferred_element_type=jnp.float32,
        )
        return (normed_rows, logit_rows.reshape(8, chain_positions_local, head_count))

    pair_normed, logits = lax.map(
        norm_rows, contact_matrix.reshape(row_blocks, 8, chain_positions_local, pair_width)
    )
    logits = jnp.where(
        res_valid[None, :, None],
        logits.reshape(rows_dev, chain_positions_local, head_count),
        MASKED,
    )
    logits = logits.transpose(0, 2, 1)
    peak = lax.pmax(jnp.max(logits, axis=2), "col")
    expo = jnp.exp(logits - peak[:, :, None])
    totals = lax.psum(jnp.sum(expo, axis=2), "col")
    local_weights = (expo / totals[:, :, None]).astype(jnp.bfloat16)
    part_rows = rows_dev // lax.axis_size("row")
    sectioned = local_weights.reshape(1, rows_dev, head_count, 1, chain_positions_local)
    moved = lax.all_to_all(
        lax.all_to_all(sectioned, "row", split_axis=1, concat_axis=0, tiled=True),
        "col",
        split_axis=0,
        concat_axis=3,
        tiled=True,
    )
    moved = moved.reshape(
        ratio, part_rows, head_count, lax.axis_size("col") * chain_positions_local
    )
    mine = lax.all_gather(moved, "row", axis=1, tiled=True).reshape(
        chain_positions_local, head_count, lax.axis_size("col") * chain_positions_local
    )
    value_weight = mixing_value_gate_matrix[0][:, :hidden_width]
    gate_weight = mixing_value_gate_matrix[0][:, hidden_width:]
    gate = jax.nn.sigmoid(
        jnp.dot(reshaped_tensor, gate_weight, preferred_element_type=jnp.float32)
    ).reshape(homolog_rows_local, chain_positions_local, hidden_width)
    values_local = jnp.dot(reshaped_tensor, value_weight, preferred_element_type=jnp.float32)
    values_local = values_local.astype(jnp.bfloat16).reshape(
        homolog_rows_local, chain_positions_local, hidden_width
    )
    values_piece = lax.all_gather(values_local, "col", axis=1, tiled=True)
    count = values_piece.shape[1]
    heads_piece = values_piece.reshape(homolog_rows_local, count, head_count, head_width)
    averaged = jnp.einsum("ihj,sjhc->sihc", mine, heads_piece, preferred_element_type=jnp.float32)
    gated = (
        gate * averaged.reshape(homolog_rows_local, chain_positions_local, hidden_width)
    ).astype(jnp.bfloat16)
    contact_increment = jnp.dot(
        gated.reshape(homolog_rows_local * chain_positions_local, hidden_width),
        mixing_final_matrix[0],
        preferred_element_type=jnp.float32,
    )
    homolog_matrix = (
        homolog_matrix.astype(jnp.float32)
        + contact_increment.reshape(homolog_rows_local, chain_positions_local, homolog_rows_full)
    ).astype(jnp.bfloat16)
    up_weight = feedforward_gate_expand[0]
    down_weight = feedforward_shrink_matrix[0]

    def transition_rows(inputs):
        pair_rows, normed_rows = inputs
        hidden = jnp.dot(
            normed_rows.reshape(8 * chain_positions_local, pair_width),
            up_weight,
            preferred_element_type=jnp.float32,
        )
        active = (jax.nn.silu(hidden[:, :trans_width]) * hidden[:, trans_width:]).astype(
            jnp.bfloat16
        )
        update = jnp.dot(active, down_weight, preferred_element_type=jnp.float32)
        return (
            pair_rows.astype(jnp.float32) + update.reshape(8, chain_positions_local, pair_width)
        ).astype(jnp.bfloat16)

    contact_matrix = lax.map(
        transition_rows,
        (contact_matrix.reshape(row_blocks, 8, chain_positions_local, pair_width), pair_normed),
    )
    contact_matrix = contact_matrix.reshape(rows_dev, chain_positions_local, pair_width)
    return (homolog_matrix, contact_matrix)


def solution(mesh):
    in_specs = (
        P("row", "col", None),
        P("row", "col", None),
        P(),
        P(),
        P(),
        P(),
        P(),
        P(),
        P(),
        P(),
        P(),
    )
    out_specs = (P("row", "col", None), P("row", "col", None))
    return jax.shard_map(local, mesh=mesh, in_specs=in_specs, out_specs=out_specs, check_vma=False)
```

profile of v0, /device:TPU:0, one launch (start us, length us, event | category | flops | bytes accessed | tf_op | source)
XLA Modules:
  0.0 227.5 jit_solution(14530378645405625014)
XLA Ops:
  8.5 0.9 convert_reduce_fusion.1
  9.5 1.0 fusion.39
  10.5 0.9 fusion.40
  11.5 0.9 fusion.35
  12.8 33.5 %all_gather.10 = bf16[64,5120]{1,0:T(8,128)(2,1)S(1)} all-gather(bf16[8,5120]{1,0:T(8,128)(2,1)S(1)} %reshape.211), channel_id=1, replica_groups=mesh['row'=8,'col'=4] {'row'}, dimensions={0}, use_global_device_ids=true | all-gather | bytes 737280 | tf_op jit(solution)/shard_map/all_gather | solution.py:70
  46.3 0.8 reshape.212
  47.1 1.5 fusion.49
  48.8 0.8 copy.53
  49.8 39.0 %all-reduce.2.cloned.1.call-done = bf16[64,80,32]{2,1,0:T(8,128)(2,1)} async-done(((bf16[64,80,32]{2,1,0:T(8,128)(2,1)}), bf16[64,80,32]{2,1,0:T(8,128)(2,1)}) %all-reduce.2.cloned.1.call-update) | async-done | bytes 327696 | tf_op jit(solution)/shard_map/psum | solution.py:12
  88.9 1.2 constant_dynamic-slice_fusion.2
  90.0 0.4 copy.54
  90.6 43.2 %while.32 = (s32[]{:T(128)}, bf16[5,8,80,128]{3,2,1,0:T(8,128)(2,1)S(1)}, bf16[5,8,80,128]{3,2,1,0:T(8,128)(2,1)}, s32[5]{0:T(128)S(1)}, bf16[64,40,32]{0,2,1:T(...) while((s32[]{:T(128)}, ...), condition=%wide.region_4.5_spmd, body=%wide.region_3.4_spmd.sunk | while | flops 253214720 | bytes 15736487 | solution.py:102
  90.6 0.7 dynamic_slice.57
  93.3 0.7 copy.72
  94.0 0.7 convolution_bitcast_fusion.3
  94.7 2.4 %copy.73 = f32[8,80,32,32]{1,3,2,0:T(8,128)S(1)} copy(f32[8,80,32,32]{1,2,3,0:T(8,128)S(1)} %convolution_bitcast_fusion.3) | data formatting | bytes 5242880 | tf_op jit(solution)/shard_map/while/body/eval_jaxpr/transpose | solution.py:87
  97.5 1.7 fusion.83
  99.2 0.7 dynamic_slice.57
  101.9 0.7 copy.72
  102.7 0.7 convolution_bitcast_fusion.3
  103.4 2.4 %copy.73 = f32[8,80,32,32]{1,3,2,0:T(8,128)S(1)} copy(f32[8,80,32,32]{1,2,3,0:T(8,128)S(1)} %convolution_bitcast_fusion.3) | data formatting | bytes 5242880 | tf_op jit(solution)/shard_map/while/body/eval_jaxpr/transpose | solution.py:87
  106.1 1.7 fusion.83
  107.8 0.7 dynamic_slice.57
  110.6 0.7 copy.72
  111.3 0.7 convolution_bitcast_fusion.3
  112.0 2.4 %copy.73 = f32[8,80,32,32]{1,3,2,0:T(8,128)S(1)} copy(f32[8,80,32,32]{1,2,3,0:T(8,128)S(1)} %convolution_bitcast_fusion.3) | data formatting | bytes 5242880 | tf_op jit(solution)/shard_map/while/body/eval_jaxpr/transpose | solution.py:87
  114.8 1.7 fusion.83
  116.5 0.7 dynamic_slice.57
  119.2 0.7 copy.72
  119.9 0.7 convolution_bitcast_fusion.3
  120.6 2.4 %copy.73 = f32[8,80,32,32]{1,3,2,0:T(8,128)S(1)} copy(f32[8,80,32,32]{1,2,3,0:T(8,128)S(1)} %convolution_bitcast_fusion.3) | data formatting | bytes 5242880 | tf_op jit(solution)/shard_map/while/body/eval_jaxpr/transpose | solution.py:87
  123.4 1.7 fusion.83
  125.1 0.7 dynamic_slice.57
  127.8 0.7 copy.72
  128.6 0.7 convolution_bitcast_fusion.3
  129.3 2.4 %copy.73 = f32[8,80,32,32]{1,3,2,0:T(8,128)S(1)} copy(f32[8,80,32,32]{1,2,3,0:T(8,128)S(1)} %convolution_bitcast_fusion.3) | data formatting | bytes 5242880 | tf_op jit(solution)/shard_map/while/body/eval_jaxpr/transpose | solution.py:87
  132.0 1.7 fusion.83
  133.9 5.9 %while.33 = (s32[]{:T(128)}, bf16[5,8,80,128]{3,2,1,0:T(8,128)(2,1)S(1)}, f32[5,8,80,8]{2,3,1,0:T(8,128)S(1)}, bf16[5,8,80,128]{3,2,1,0:T(8,128)(2,1)S(1)}, bf16[128,8]{0,1:T(8,128)(2,1)S(1)}, /*index=5*/s32[]{:T(128)}) while((s32[]{:T(128)}, bf16[5,8,80,128]{3,2,1,0:T(8,128)(2,1)S(1)}, f32[5,8,80,8]{2,3,1,0:T(8,128)S(1)}, ...), condition=%wide.region_8.9_spmd, body=%wide.region_5.8_spmd.sunk | while | flops 2458242 | bytes 889425 | solution.py:117
  134.7 0.4 fusion.88
  139.9 10.4 %pmax.7 = f32[40,8]{1,0:T(8,128)S(1)} all-reduce(f32[40,8]{1,0:T(8,128)S(1)} %bitcast_reduce_fusion), channel_id=1, replica_groups=mesh['row'=8,'col'=4] {'col'}, use_global_device_ids=true, to_apply=%region_10.11 | all-reduce | flops 320 | bytes 2560 | tf_op jit(solution)/shard_map/pmax | solution.py:126
  150.5 10.3 %psum.15 = f32[40,8]{1,0:T(8,128)S(1)} all-reduce(f32[40,8]{1,0:T(8,128)S(1)} %fusion.42), channel_id=1, replica_groups=mesh['row'=8,'col'=4] {'col'}, use_global_device_ids=true, to_apply=%region_12.13 | all-reduce | flops 320 | bytes 2560 | tf_op jit(solution)/shard_map/psum | solution.py:128
  160.7 0.8 fusion.43
  161.5 5.6 %all-to-all-start = ((bf16[1,40,8,1,80]{4,2,3,0,1:T(8,128)(2,1)}), bf16[1,40,8,1,80]{4,2,3,0,1:T(8,128)(2,1)}, u32[]{:S(2)}, u32[]{:S(2)}) async-start(bf16[1,40,8,1,80]{4,2,3,0,1:T(8,128)(2,1)} %fusion.43), calls=%async_computation | async-start | bytes 163840 | tf_op jit(solution)/shard_map/all_to_all | solution.py:133
  167.5 0.8 copy.49
  168.4 5.9 %all-to-all-done = bf16[1,40,8,1,80]{4,2,3,0,1:T(8,128)(2,1)} async-done(((bf16[1,40,8,1,80]{4,2,3,0,1:T(8,128)(2,1)}), bf16[1,40,8,1,80]{4,2,3,0,1:T(8,128)(2,1)}, u32[]{:S(2)}, u32[]{:S(2)}) %all-to-all-start) | async-done | bytes 51232 | tf_op jit(solution)/shard_map/all_to_all | solution.py:133
  174.3 3.5 %all-to-all-start.1 = ((bf16[8,5,8,1,80]{4,2,1,3,0:T(8,128)(2,1)}), bf16[8,5,8,1,80]{4,2,1,3,0:T(8,128)(2,1)S(1)}, u32[]{:S(2)}, u32[]{:S(2)}) async-start(bf16[8,5,8,1,80]{4,2,1,3,0:T(8,128)(2,1)} %bitcast.35), calls=%async_computation.1 | async-start | bytes 163840 | tf_op jit(solution)/shard_map/all_to_all | solution.py:132
  177.9 5.4 %while.34 = (s32[]{:T(128)}, bf16[5,8,80,128]{3,2,1,0:T(8,128)(2,1)S(1)}, bf16[5,8,80,128]{3,2,1,0:T(8,128)(2,1)S(1)}, bf16[5,8,80,128]{3,2,1,0:T(8,128)(2,1)S(1...) while((s32[]{:T(128)}, bf16[5,8,80,128]{3,2,1,0:T(8,128)(2,1)S(1)}, ...), condition=%wide.region_14.15_spmd, body=%wide.region_13.14_spmd.sunk | while | flops 253870080 | bytes 7110741 | solution.py:188
  177.9 0.5 fusion.93
  178.4 0.5 fusion.94
  179.0 0.5 fusion.93
  179.5 0.5 fusion.94
  180.1 0.5 fusion.93
  180.6 0.5 fusion.94
  181.2 0.5 fusion.93
  181.7 0.5 fusion.94
  182.3 0.5 fusion.93
  182.8 0.5 fusion.94
  183.5 31.5 %all_gather.11 = bf16[2,40,8,320]{3,2,1,0:T(8,128)(2,1)S(1)} all-gather(bf16[2,5,8,320]{3,2,1,0:T(8,128)(2,1)S(1)} %reshape.217), channel_id=1, replica_groups=mesh['row'=8,'col'=4] {'row'}, dimensions={1}, use_global_device_ids=true | all-gather | bytes 460800 | tf_op jit(solution)/shard_map/all_gather | solution.py:142
  215.1 2.0 copy.50
  217.1 0.6 fusion.27
  217.6 0.6 copy.59
  218.8 0.4 fusion.34
  219.2 0.5 copy-done.3
  219.7 0.9 fusion.36
  (94 shorter events, 10.1 us)
Async XLA Ops:
  7.2 212.0 %copy-start = (bf16[1,256,64]{1,2,0:T(8,128)(2,1)S(1)}, bf16[1,256,64]{1,2,0:T(8,128)(2,1)}, u32[]{:S(2)}) copy-start(bf16[1,256,64]{1,2,0:T(8,128)(2,1)} %param.25) | copy-start | bytes 98308
  7.2 81.7 %all-reduce.2.cloned.1.call-start = ((), (), s32[]{:S(2)}) async-start(), calls=%async_computation.3 | async-start | bytes 2621440 | tf_op jit(solution)/shard_map/psum | solution.py:12
  49.8 40.7 %copy-start.1 = (bf16[1,1024,128]{2,1,0:T(8,128)(2,1)S(1)}, bf16[1,1024,128]{2,1,0:T(8,128)(2,1)}, u32[]{:S(2)}) copy-start(bf16[1,1024,128]{2,1,0:T(8,128)(2,1)} %param.22) | copy-start | bytes 786436
  90.5 43.3 %copy-start.7 = (bf16[1,128,8]{1,2,0:T(8,128)(2,1)S(1)}, bf16[1,128,8]{1,2,0:T(8,128)(2,1)}, u32[]{:S(2)}) copy-start(bf16[1,128,8]{1,2,0:T(8,128)(2,1)} %param.24) | copy-start | bytes 6148
  133.9 33.4 %copy-start.5 = (bf16[1,64,512]{2,1,0:T(8,128)(2,1)S(1)}, bf16[1,64,512]{2,1,0:T(8,128)(2,1)}, u32[]{:S(2)}) copy-start(bf16[1,64,512]{2,1,0:T(8,128)(2,1)} %param.23) | copy-start | bytes 196612
  139.9 38.0 %copy-start.2 = (bf16[1,128,1024]{2,1,0:T(8,128)(2,1)S(1)}, bf16[1,128,1024]{2,1,0:T(8,128)(2,1)}, u32[]{:S(2)}) copy-start(bf16[1,128,1024]{2,1,0:T(8,128)(2,1)} %param.26) | copy-start | bytes 786436
  139.9 38.0 %copy-start.6 = (bf16[1,512,128]{2,1,0:T(8,128)(2,1)S(1)}, bf16[1,512,128]{2,1,0:T(8,128)(2,1)}, u32[]{:S(2)}) copy-start(bf16[1,512,128]{2,1,0:T(8,128)(2,1)} %param.27) | copy-start | bytes 393220
  161.5 12.7 %all-to-all-start = ((bf16[1,40,8,1,80]{4,2,3,0,1:T(8,128)(2,1)}), bf16[1,40,8,1,80]{4,2,3,0,1:T(8,128)(2,1)}, u32[]{:S(2)}, u32[]{:S(2)}) async-start(bf16[1,40,8,1,80]{4,2,3,0,1:T(8,128)(2,1)} %fusion.43), calls=%async_computation | async-start | bytes 163840 | tf_op jit(solution)/shard_map/all_to_all | solution.py:133
  167.2 47.9 %all-gather.2.cloned.1.call-start = ((), (), s32[]{:S(2)}) async-start(), calls=%async_computation.2 | async-start | bytes 1638400 | tf_op jit(solution)/shard_map/all_gather | solution.py:154
  174.3 9.1 %all-to-all-start.1 = ((bf16[8,5,8,1,80]{4,2,1,3,0:T(8,128)(2,1)}), bf16[8,5,8,1,80]{4,2,1,3,0:T(8,128)(2,1)S(1)}, u32[]{:S(2)}, u32[]{:S(2)}) async-start(bf16[8,5,8,1,80]{4,2,1,3,0:T(8,128)(2,1)} %bitcast.35), calls=%async_computation.1 | async-start | bytes 163840 | tf_op jit(solution)/shard_map/all_to_all | solution.py:132
  183.3 33.7 %copy-start.4 = (bf16[5,8,80,128]{3,2,1,0:T(8,128)(2,1)}, bf16[5,8,80,128]{3,2,1,0:T(8,128)(2,1)S(1)}, u32[]{:S(2)}) copy-start(bf16[5,8,80,128]{3,2,1,0:T(8,128)(2,1)S(1)} %get-tuple-element.107) | copy-start | bytes 2457604
  218.8 0.9 copy-start.3
Sparse Core Ops, SparseCore 0:
  48.8 40.0 all-reduce.1
  169.5 19.9 all-gather.1
where the time goes:
time: 228 us; the launch traced here: 227 us
  blocking collectives  85.6 us (38%)
  waiting for transfers between devices  45 us (20%)
  local copies, waits for them, and re-layouts  27.9 us (12%)
  matrix products  21.6 us (9%)
  between operations  15.7 us (7%)
  other arithmetic  11.6 us (5%)
  loops' own time  10.9 us (5%)
  starting transfers between devices  9.17 us (4%)
    psum x1, waiting for transfers between devices, broadcast(): return lax.psum(kept, axis)  39 us
    all_gather x1, blocking collectives, local(): lax.all_gather(packed, 'row', axis=0, tiled=True)  33.5 us
    all_gather x1, blocking collectives, local(): lax.all_gather(moved, 'row', axis=1, tiled=True)  31.5 us
    transpose x5, local copies, waits for them, and re-layouts, outer_rows(): product.reshape(8, outer_width, chain_positions_local, outer_width)  11.9 us
    another operation x1, loops' own time, local(): lax.map(outer_rows, (starts, contact_matrix.reshape(row_blocks, 8, chain_...  10.6 us
    pmax x1, blocking collectives, local(): peak = lax.pmax(jnp.max(logits, axis=2), 'col')  10.4 us
    psum x1, blocking collectives, local(): totals = lax.psum(jnp.sum(expo, axis=2), 'col')  10.3 us
    dot_general x5, matrix products, outer_rows(): jnp.dot(outer.reshape(8 * chain_positions_local, outer_width * outer_widt...  8.51 us
  transfers between devices with their start and end apart: 4, of which 2 were waited for; matrix products, arithmetic and copies ran while one was open for 3% of the time, Pallas kernels for 0%

commit v1 on v0

--- a/solution.py
+++ b/solution.py
@@ -9,7 +9,10 @@
 
 def broadcast(value, axis, source):
     kept = jnp.where(lax.axis_index(axis) == source, value, 0).astype(value.dtype)
-    return lax.psum(kept, axis)
+    _match_rings = lambda local_block, axis_id: jnp.sum(
+        lax.all_gather(local_block, axis_id), axis=0
+    )
+    return _match_rings(kept, axis)
 
 
 def standardize_features(field):

time: 228 us -> 217 us (0.952)
  waiting for transfers between devices: 45 us -> 30.8 us
    psum x1 -> x0, waiting for transfers between devices: 39 us -> none  [broadcast(): return lax.psum(kept, axis)]
    all_gather x0 -> x1, waiting for transfers between devices: none -> 18 us  [broadcast(): lax.all_gather(local_block, axis_id)]
    all_gather x1, waiting for transfers between devices: 0.02 us -> 6.78 us  [local(): values_piece = lax.all_gather(values_local, 'col', axis=1, tiled=True)]
    select_n x0 -> x2, local copies, waits for them, and re-layouts: none -> 2.77 us  [broadcast(): jnp.where(lax.axis_index(axis) == source, value, 0).astype(value.dtype)]
  transfers between devices with their start and end apart: 4 -> 4, of which waited for: 2 -> 3; matrix products, arithmetic and copies ran while one was open for 3% -> 4% of each run, Pallas kernels for 0% -> 0%
where the time goes in v1:
time: 217 us; the launch traced here: 216 us
  blocking collectives  85.7 us (39%)
  waiting for transfers between devices  30.8 us (14%)
  local copies, waits for them, and re-layouts  29.5 us (14%)
  matrix products  21.6 us (10%)
  between operations  15.7 us (7%)
  other arithmetic  13.2 us (6%)
  loops' own time  10.3 us (5%)
  starting transfers between devices  9.19 us (4%)
    all_gather x1, blocking collectives, local(): lax.all_gather(packed, 'row', axis=0, tiled=True)  33.5 us
    all_gather x1, blocking collectives, local(): lax.all_gather(moved, 'row', axis=1, tiled=True)  31.5 us
    all_gather x1, waiting for transfers between devices, broadcast(): lax.all_gather(local_block, axis_id)  18 us
    transpose x5, local copies, waits for them, and re-layouts, outer_rows(): product.reshape(8, outer_width, chain_positions_local, outer_width)  11.9 us
    pmax x1, blocking collectives, local(): peak = lax.pmax(jnp.max(logits, axis=2), 'col')  10.5 us
    psum x1, blocking collectives, local(): totals = lax.psum(jnp.sum(expo, axis=2), 'col')  10.3 us
    another operation x1, loops' own time, local(): lax.map(outer_rows, (starts, contact_matrix.reshape(row_blocks, 8, chain_...  9.93 us
    dot_general x5, matrix products, outer_rows(): jnp.dot(outer.reshape(8 * chain_positions_local, outer_width * outer_widt...  8.51 us
  transfers between devices with their start and end apart: 4, of which 3 were waited for; matrix products, arithmetic and copies ran while one was open for 4% of the time, Pallas kernels for 0%

profile of v1, /device:TPU:0, one launch (start us, length us, event | category | flops | bytes accessed | tf_op | source)
XLA Modules:
  0.0 215.9 jit_solution(5196573323671197689)
XLA Ops:
  8.5 0.9 convert_reduce_fusion.1
  9.5 1.0 fusion.39
  10.5 0.9 fusion.40
  11.5 0.9 fusion.35
  12.8 33.5 %all_gather.14 = bf16[64,5120]{1,0:T(8,128)(2,1)S(1)} all-gather(bf16[8,5120]{1,0:T(8,128)(2,1)S(1)} %reshape.221), channel_id=1, replica_groups=mesh['row'=8,'col'=4] {'row'}, dimensions={0}, use_global_device_ids=true | all-gather | bytes 737280 | tf_op jit(solution)/shard_map/all_gather | solution.py:73
  46.3 0.8 reshape.222
  47.1 1.5 fusion.49
  48.6 1.8 copy.73
  50.4 1.0 copy.74
  51.5 0.8 copy.76
  52.6 18.0 %all-gather.5.cloned.1.call-done = bf16[4,64,2560]{2,1,0:T(8,128)(2,1)} async-done(((bf16[1,64,2560]{2,1,0:T(8,128)(2,1)}), bf16[4,64,2560]{2,1,0:T(8,128)(2,1)}) %all-gather.5.cloned.1.call-update) | async-done | bytes 1310736 | tf_op jit(solution)/shard_map/all_gather | solution.py:13
  70.7 1.5 reduce_sum.59
  73.1 42.1 %while.32 = (s32[]{:T(128)}, bf16[5,8,80,128]{3,2,1,0:T(8,128)(2,1)S(1)}, bf16[5,8,80,128]{3,2,1,0:T(8,128)(2,1)}, s32[5]{0:T(128)S(1)}, bf16[64,40,32]{0,2,1:T(...) while((s32[]{:T(128)}, ...), condition=%wide.region_4.5_spmd, body=%wide.region_3.4_spmd.sunk | while | flops 253214720 | bytes 15736487 | solution.py:105
  73.1 0.6 dynamic_slice.57
  75.7 0.7 copy.94
  76.4 0.7 convolution_bitcast_fusion.3
  77.1 2.4 %copy.95 = f32[8,80,32,32]{1,3,2,0:T(8,128)S(1)} copy(f32[8,80,32,32]{1,2,3,0:T(8,128)S(1)} %convolution_bitcast_fusion.3) | data formatting | bytes 5242880 | tf_op jit(solution)/shard_map/while/body/eval_jaxpr/transpose | solution.py:90
  79.8 1.7 fusion.83
  81.6 0.6 dynamic_slice.57
  84.1 0.7 copy.94
  84.8 0.7 convolution_bitcast_fusion.3
  85.5 2.4 %copy.95 = f32[8,80,32,32]{1,3,2,0:T(8,128)S(1)} copy(f32[8,80,32,32]{1,2,3,0:T(8,128)S(1)} %convolution_bitcast_fusion.3) | data formatting | bytes 5242880 | tf_op jit(solution)/shard_map/while/body/eval_jaxpr/transpose | solution.py:90
  88.3 1.7 fusion.83
  90.0 0.6 dynamic_slice.57
  92.5 0.7 copy.94
  93.2 0.7 convolution_bitcast_fusion.3
  93.9 2.4 %copy.95 = f32[8,80,32,32]{1,3,2,0:T(8,128)S(1)} copy(f32[8,80,32,32]{1,2,3,0:T(8,128)S(1)} %convolution_bitcast_fusion.3) | data formatting | bytes 5242880 | tf_op jit(solution)/shard_map/while/body/eval_jaxpr/transpose | solution.py:90
  96.7 1.7 fusion.83
  98.4 0.6 dynamic_slice.57
  100.9 0.7 copy.94
  101.7 0.7 convolution_bitcast_fusion.3
  102.3 2.4 %copy.95 = f32[8,80,32,32]{1,3,2,0:T(8,128)S(1)} copy(f32[8,80,32,32]{1,2,3,0:T(8,128)S(1)} %convolution_bitcast_fusion.3) | data formatting | bytes 5242880 | tf_op jit(solution)/shard_map/while/body/eval_jaxpr/transpose | solution.py:90
  105.1 1.7 fusion.83
  106.8 0.6 dynamic_slice.57
  109.3 0.7 copy.94
  110.1 0.7 convolution_bitcast_fusion.3
  110.8 2.4 %copy.95 = f32[8,80,32,32]{1,3,2,0:T(8,128)S(1)} copy(f32[8,80,32,32]{1,2,3,0:T(8,128)S(1)} %convolution_bitcast_fusion.3) | data formatting | bytes 5242880 | tf_op jit(solution)/shard_map/while/body/eval_jaxpr/transpose | solution.py:90
  113.5 1.7 fusion.83
  115.4 5.9 %while.33 = (s32[]{:T(128)}, bf16[5,8,80,128]{3,2,1,0:T(8,128)(2,1)S(1)}, f32[5,8,80,8]{2,3,1,0:T(8,128)S(1)}, bf16[5,8,80,128]{3,2,1,0:T(8,128)(2,1)S(1)}, bf16[128,8]{0,1:T(8,128)(2,1)S(1)}, /*index=5*/s32[]{:T(128)}) while((s32[]{:T(128)}, bf16[5,8,80,128]{3,2,1,0:T(8,128)(2,1)S(1)}, f32[5,8,80,8]{2,3,1,0:T(8,128)S(1)}, ...), condition=%wide.region_8.9_spmd, body=%wide.region_5.8_spmd.sunk | while | flops 2458242 | bytes 889425 | solution.py:120
  121.4 10.5 %pmax.7 = f32[40,8]{1,0:T(8,128)S(1)} all-reduce(f32[40,8]{1,0:T(8,128)S(1)} %bitcast_reduce_fusion), channel_id=1, replica_groups=mesh['row'=8,'col'=4] {'col'}, use_global_device_ids=true, to_apply=%region_10.11 | all-reduce | flops 320 | bytes 2560 | tf_op jit(solution)/shard_map/pmax | solution.py:129
  132.1 10.3 %psum.7 = f32[40,8]{1,0:T(8,128)S(1)} all-reduce(f32[40,8]{1,0:T(8,128)S(1)} %fusion.42), channel_id=1, replica_groups=mesh['row'=8,'col'=4] {'col'}, use_global_device_ids=true, to_apply=%region_12.13 | all-reduce | flops 320 | bytes 2560 | tf_op jit(solution)/shard_map/psum | solution.py:131
  142.3 0.8 fusion.43
  143.1 5.6 %all-to-all-start = ((bf16[1,40,8,1,80]{4,2,3,0,1:T(8,128)(2,1)}), bf16[1,40,8,1,80]{4,2,3,0,1:T(8,128)(2,1)}, u32[]{:S(2)}, u32[]{:S(2)}) async-start(bf16[1,40,8,1,80]{4,2,3,0,1:T(8,128)(2,1)} %fusion.43), calls=%async_computation | async-start | bytes 163840 | tf_op jit(solution)/shard_map/all_to_all | solution.py:136
  149.1 0.8 copy.69
  150.0 5.9 %all-to-all-done = bf16[1,40,8,1,80]{4,2,3,0,1:T(8,128)(2,1)} async-done(((bf16[1,40,8,1,80]{4,2,3,0,1:T(8,128)(2,1)}), bf16[1,40,8,1,80]{4,2,3,0,1:T(8,128)(2,1)}, u32[]{:S(2)}, u32[]{:S(2)}) %all-to-all-start) | async-done | bytes 51232 | tf_op jit(solution)/shard_map/all_to_all | solution.py:136
  155.9 3.5 %all-to-all-start.1 = ((bf16[8,5,8,1,80]{4,2,1,3,0:T(8,128)(2,1)}), bf16[8,5,8,1,80]{4,2,1,3,0:T(8,128)(2,1)S(1)}, u32[]{:S(2)}, u32[]{:S(2)}) async-start(bf16[8,5,8,1,80]{4,2,1,3,0:T(8,128)(2,1)} %bitcast.37), calls=%async_computation.1 | async-start | bytes 163840 | tf_op jit(solution)/shard_map/all_to_all | solution.py:135
  159.5 5.4 %while.34 = (s32[]{:T(128)}, bf16[5,8,80,128]{3,2,1,0:T(8,128)(2,1)S(1)}, bf16[5,8,80,128]{3,2,1,0:T(8,128)(2,1)S(1)}, bf16[5,8,80,128]{3,2,1,0:T(8,128)(2,1)S(1...) while((s32[]{:T(128)}, bf16[5,8,80,128]{3,2,1,0:T(8,128)(2,1)S(1)}, ...), condition=%wide.region_14.15_spmd, body=%wide.region_13.14_spmd.sunk | while | flops 253870080 | bytes 7110741 | solution.py:191
  159.5 0.5 fusion.93
  160.0 0.5 fusion.94
  160.6 0.5 fusion.93
  161.1 0.5 fusion.94
  161.7 0.5 fusion.93
  162.2 0.5 fusion.94
  162.8 0.5 fusion.93
  163.3 0.5 fusion.94
  163.9 0.5 fusion.93
  164.4 0.5 fusion.94
  164.9 6.8 %all-gather.3.cloned.1.call-done = bf16[8,320,256]{2,0,1:T(8,128)(2,1)} async-done(((bf16[8,80,256]{2,0,1:T(8,128)(2,1)}), bf16[8,320,256]{2,0,1:T(8,128)(2,1)}) %all-gather.3.cloned.1.call-update) | async-done | bytes 1310736 | tf_op jit(solution)/shard_map/all_gather | solution.py:157
  171.7 2.0 copy.70
  173.9 31.5 %all_gather.16 = bf16[2,40,8,320]{3,2,1,0:T(8,128)(2,1)S(1)} all-gather(bf16[2,5,8,320]{3,2,1,0:T(8,128)(2,1)S(1)} %reshape.227), channel_id=1, replica_groups=mesh['row'=8,'col'=4] {'row'}, dimensions={1}, use_global_device_ids=true | all-gather | bytes 460800 | tf_op jit(solution)/shard_map/all_gather | solution.py:145
  205.4 0.6 fusion.27
  206.0 0.6 copy.81
  207.6 0.5 copy-done.3
  208.1 0.9 fusion.36
  (97 shorter events, 11.6 us)
Async XLA Ops:
  7.2 200.4 %copy-start = (bf16[1,256,64]{1,2,0:T(8,128)(2,1)S(1)}, bf16[1,256,64]{1,2,0:T(8,128)(2,1)}, u32[]{:S(2)}) copy-start(bf16[1,256,64]{1,2,0:T(8,128)(2,1)} %param.25) | copy-start | bytes 98308
  7.2 63.5 %all-gather.5.cloned.1.call-start = ((), (), s32[]{:S(2)}) async-start(), calls=%async_computation.3 | async-start | bytes 1638400 | tf_op jit(solution)/shard_map/all_gather | solution.py:13
  72.2 1.0 copy-start.1
  73.1 42.2 %copy-start.7 = (bf16[1,128,8]{1,2,0:T(8,128)(2,1)S(1)}, bf16[1,128,8]{1,2,0:T(8,128)(2,1)}, u32[]{:S(2)}) copy-start(bf16[1,128,8]{1,2,0:T(8,128)(2,1)} %param.24) | copy-start | bytes 6148
  115.4 33.4 %copy-start.5 = (bf16[1,64,512]{2,1,0:T(8,128)(2,1)S(1)}, bf16[1,64,512]{2,1,0:T(8,128)(2,1)}, u32[]{:S(2)}) copy-start(bf16[1,64,512]{2,1,0:T(8,128)(2,1)} %param.23) | copy-start | bytes 196612
  121.4 38.1 %copy-start.2 = (bf16[1,128,1024]{2,1,0:T(8,128)(2,1)S(1)}, bf16[1,128,1024]{2,1,0:T(8,128)(2,1)}, u32[]{:S(2)}) copy-start(bf16[1,128,1024]{2,1,0:T(8,128)(2,1)} %param.26) | copy-start | bytes 786436
  121.4 38.1 %copy-start.6 = (bf16[1,512,128]{2,1,0:T(8,128)(2,1)S(1)}, bf16[1,512,128]{2,1,0:T(8,128)(2,1)}, u32[]{:S(2)}) copy-start(bf16[1,512,128]{2,1,0:T(8,128)(2,1)} %param.27) | copy-start | bytes 393220
  143.1 12.8 %all-to-all-start = ((bf16[1,40,8,1,80]{4,2,3,0,1:T(8,128)(2,1)}), bf16[1,40,8,1,80]{4,2,3,0,1:T(8,128)(2,1)}, u32[]{:S(2)}, u32[]{:S(2)}) async-start(bf16[1,40,8,1,80]{4,2,3,0,1:T(8,128)(2,1)} %fusion.43), calls=%async_computation | async-start | bytes 163840 | tf_op jit(solution)/shard_map/all_to_all | solution.py:136
  148.8 22.9 %all-gather.3.cloned.1.call-start = ((), (), s32[]{:S(2)}) async-start(), calls=%async_computation.2 | async-start | bytes 1638400 | tf_op jit(solution)/shard_map/all_gather | solution.py:157
  155.9 17.8 %all-to-all-start.1 = ((bf16[8,5,8,1,80]{4,2,1,3,0:T(8,128)(2,1)}), bf16[8,5,8,1,80]{4,2,1,3,0:T(8,128)(2,1)S(1)}, u32[]{:S(2)}, u32[]{:S(2)}) async-start(bf16[8,5,8,1,80]{4,2,1,3,0:T(8,128)(2,1)} %bitcast.37), calls=%async_computation.1 | async-start | bytes 163840 | tf_op jit(solution)/shard_map/all_to_all | solution.py:135
  164.9 9.0 %copy-start.4 = (bf16[5,8,80,128]{3,2,1,0:T(8,128)(2,1)}, bf16[5,8,80,128]{3,2,1,0:T(8,128)(2,1)S(1)}, u32[]{:S(2)}) copy-start(bf16[5,8,80,128]{3,2,1,0:T(8,128)(2,1)S(1)} %get-tuple-element.107) | copy-start | bytes 2457604
  207.2 0.9 copy-start.3
Sparse Core Ops, SparseCore 0:
  51.5 19.0 all-gather.4
  151.1 20.5 all-gather.2
